TPU v7x, 32 devices: a whole 2x2x4 slice. The times are simulated.
32 devices in a mesh: wide: 8 (over y, x, core), by: 4 (over z).
Axes of the slice: x: 2, y: 2, z: 4, core: 2. Of those that a mesh axis runs over, the one named last changes fastest.
Arguments:
- tiles: float32 [704, 512, 512], P(('wide', 'by')), may hold values from -6 to 6
- tile_rows: int32 [704], P(('wide', 'by')), may hold values from 0 to 7
- tile_cols: int32 [704], P(('wide', 'by')), may hold values from 0 to 63, as said below
- start_panel: float32 [32768, 64], P('wide'), may hold values from -6 to 6
Outputs:
- panel: float32 [32768, 64], P('wide')
- factor: float32 [64, 64], replicated
Inputs may be any that keep to these rules, and one draw needn't show every extreme that they name: `tile_cols`: within one device's 22 tiles, at most 3 have block columns in the block rows of one index of wide, and one index of wide takes exactly 3 of them.
All inputs are finite; a program needn't handle non-finite values.
Results may differ from a plain program's by a relative error of at most 0.0001.
Values sent between devices are 32-bit elements; how exact they have to be, the bound alone decides.
No kernel may reach another device: no remote copies, remote signals or barrier semaphores. Data moves between devices by JAX's collectives and lax.ppermute only.
A program may use at most 192 MiB of HBM per device.

v0:
```python
import jax
import jax.numpy as jnp
from jax import lax
from jax.sharding import PartitionSpec as P

ITERS = 2


def local(tiles, tile_rows, tile_cols, start_panel):
    wide_count = lax.axis_size("wide")
    my_wide = lax.axis_index("wide")
    tile_count = tiles.shape[0]
    block_size = tiles.shape[1]
    width = start_panel.shape[1]
    block_rows = start_panel.shape[0] // block_size
    capacity = max(2, tile_count // wide_count + 1)
    slot_count = wide_count * capacity
    highest = lax.Precision.HIGHEST
    peer_index = tile_cols // block_rows
    positions = jnp.arange(tile_count, dtype=jnp.int32)
    earlier = positions[:, None] > positions[None, :]
    same_peer = peer_index[:, None] == peer_index[None, :]
    rank_within = jnp.sum((earlier & same_peer).astype(jnp.int32), axis=1)
    slot_of = peer_index * capacity + rank_within
    slot_match = slot_of[:, None] == jnp.arange(slot_count, dtype=jnp.int32)[None, :]
    slot_table = slot_match.astype(jnp.float32)
    request = jnp.sum(jnp.where(slot_match, tile_cols[:, None] + 1, 0), axis=0) - 1
    incoming = lax.all_to_all(
        request.reshape(wide_count, capacity), "wide", split_axis=0, concat_axis=0, tiled=True
    ).reshape(slot_count)
    local_in = incoming - my_wide * block_rows
    block_iota = jnp.arange(block_rows, dtype=jnp.int32)
    serve_table = (local_in[:, None] == block_iota[None, :]).astype(jnp.float32)
    row_table = (tile_rows[:, None] == block_iota[None, :]).astype(jnp.float32)
    panel = start_panel
    factor = jnp.zeros((width, width), jnp.float32)
    for step in range(ITERS):
        flat_panel = panel.reshape(block_rows, block_size * width)
        outgoing = jnp.dot(serve_table, flat_panel, precision=highest)
        received = lax.all_to_all(outgoing, "wide", split_axis=0, concat_axis=0, tiled=True)
        col_panels = jnp.dot(slot_table, received, precision=highest).reshape(
            tile_count, block_size, width
        )
        row_panels = jnp.dot(row_table, flat_panel, precision=highest).reshape(
            tile_count, block_size, width
        )
        direct = jnp.einsum("tab,tbk->tak", tiles, col_panels, precision=highest)
        mirror = jnp.einsum("tba,tbk->tak", tiles, row_panels, precision=highest)
        partial_rows = jnp.dot(
            row_table.T, direct.reshape(tile_count, block_size * width), precision=highest
        )
        mirror_flat = mirror.reshape(tile_count, block_size * width)
        placed = jnp.dot(slot_table.T, mirror_flat, precision=highest)
        returned = lax.all_to_all(placed, "wide", split_axis=0, concat_axis=0, tiled=True)
        partial_rows = partial_rows + jnp.dot(serve_table.T, returned, precision=highest)
        partial_rows = partial_rows.reshape(block_rows * block_size, width)
        image = lax.psum(partial_rows, "by")
        gram = lax.psum(jnp.dot(image.T, image, precision=highest), "wide")
        factor = jnp.linalg.cholesky(gram)
        panel = jax.scipy.linalg.solve_triangular(factor, image.T, lower=True).T
    return (panel, factor)


def solution(mesh):
    placed = (P(("wide", "by"), None, None), P(("wide", "by")), P(("wide", "by")), P("wide", None))
    return jax.shard_map(
        local, mesh=mesh, in_specs=placed, out_specs=(P("wide", None), P()), check_vma=False
    )
```

profile of v0, /device:TPU:0, one launch (start us, length us, event | category | flops | bytes accessed | tf_op | source)
XLA Modules:
  0.0 638.6 jit_solution(3037137050593948503)
XLA Ops:
  8.8 5.2 all-to-all-start
  22.6 21.3 %fusion.13 = f32[22,512,64]{1,2,0:T(8,128)} fusion(f32[22,512,512]{2,1,0:T(8,128)} %param.7, f32[22,512,64]{1,0,2:T(8,128)S(1)} %fusion.60), kind=kOutput, calls=%fused_computation.15 | convolution fusion | flops 4429185024 | bytes 28835840 | tf_op jit(solution)/shard_map/tba,tbk->tak/dot_general | solution.py:48
  43.9 5.3 copy.59
  49.2 6.3 reshape.153
  75.3 41.6 %all-to-all-done.2 = f32[8,3,32768]{2,1,0:T(4,128)} async-done(((f32[8,3,32768]{2,1,0:T(4,128)}), f32[8,3,32768]{2,1,0:T(4,128)}, u32[]{:S(2)}, u32[]{:S(2)}) %all-to-all-start.2) | async-done | bytes 3145760 | tf_op jit(solution)/shard_map/all_to_all | solution.py:54
  125.3 45.2 %all-to-all-done.1 = f32[8,3,32768]{2,1,0:T(4,128)} async-done(((f32[8,3,32768]{2,1,0:T(4,128)}), f32[8,3,32768]{2,1,0:T(4,128)}, u32[]{:S(2)}, u32[]{:S(2)}) %all-to-all-start.1) | async-done | bytes 3145760 | tf_op jit(solution)/shard_map/all_to_all | solution.py:40
  170.5 5.5 all_to_all.30
  176.0 6.4 %dot_general.80 = f32[512,64,24]{1,0,2:T(8,128)} reshape(f32[32768,24]{0,1:T(8,128)} %bitcast.82) | data formatting | bytes 6291456 | tf_op jit(solution)/shard_map/dot_general | solution.py:41
  182.4 6.6 %copy.54 = f32[512,64,24]{0,2,1:T(8,128)} copy(f32[512,64,24]{1,0,2:T(8,128)} %dot_general.80) | data formatting | bytes 6291456 | tf_op jit(solution)/shard_map/dot_general | solution.py:41
  192.6 27.3 %fusion.10 = f32[22,512,64]{1,2,0:T(8,128)} fusion(f32[22,512,512]{2,1,0:T(8,128)} %param.7, f32[22,512,64]{1,0,2:T(8,128)S(1)} %fusion.37), kind=kOutput, calls=%fused_computation.14 | convolution fusion | flops 4429185024 | bytes 28835840 | tf_op jit(solution)/shard_map/tab,tbk->tak/dot_general | solution.py:47
  219.9 5.3 copy.56
  225.3 6.5 %reshape.143 = f32[22,32768]{1,0:T(8,128)} reshape(f32[22,512,64]{2,1,0:T(8,128)} %copy.56) | data formatting | bytes 5767168 | tf_op jit(solution)/shard_map/reshape | solution.py:50
  240.5 86.1 %all-reduce.3.cloned.1.call-done = f32[4096,64]{1,0:T(8,128)} async-done(((f32[4096,64]{1,0:T(8,128)}), f32[4096,64]{1,0:T(8,128)}) %all-reduce.3.cloned.1.call-update) | async-done | bytes 1048592 | tf_op jit(solution)/shard_map/psum | solution.py:57
  326.6 5.9 fusion.68
  332.5 24.3 %psum.29 = f32[64,64]{0,1:T(8,128)S(1)} all-reduce(f32[64,64]{0,1:T(8,128)S(1)} %fusion.68), channel_id=1, replica_groups=mesh['wide'=8,'by'=4] {'wide'}, use_global_device_ids=true, to_apply=%region_3.4 | all-reduce | flops 4096 | bytes 32768 | tf_op jit(solution)/shard_map/psum | solution.py:58
  356.9 5.8 cholesky.44
  386.9 19.4 %fusion.19 = f32[22,512,64]{1,2,0:T(8,128)S(1)} fusion(f32[22,512,512]{2,1,0:T(8,128)} %param.7, f32[22,512,64]{1,0,2:T(8,128)S(1)} %fusion.58), kind=kOutput, calls=%fused_computation.17 | convolution fusion | flops 4429185024 | bytes 28835840 | tf_op jit(solution)/shard_map/tba,tbk->tak/dot_general | solution.py:48
  420.5 11.6 %all-to-all-done.3 = f32[8,3,32768]{2,1,0:T(4,128)} async-done(((f32[8,3,32768]{2,1,0:T(4,128)}), f32[8,3,32768]{2,1,0:T(4,128)}, u32[]{:S(2)}, u32[]{:S(2)}) %all-to-all-start.3) | async-done | bytes 3145760 | tf_op jit(solution)/shard_map/all_to_all | solution.py:40
  445.4 5.0 copy.65
  452.1 25.6 %fusion.16 = f32[22,512,64]{1,2,0:T(8,128)S(1)} fusion(f32[22,512,512]{2,1,0:T(8,128)} %param.7, f32[22,512,64]{1,0,2:T(8,128)S(1)} %fusion.35), kind=kOutput, calls=%fused_computation.16 | convolution fusion | flops 4429185024 | bytes 28835840 | tf_op jit(solution)/shard_map/tab,tbk->tak/dot_general | solution.py:47
  498.9 86.2 %all-reduce.5.cloned.1.call-done = f32[4096,64]{1,0:T(8,128)} async-done(((f32[4096,64]{1,0:T(8,128)}), f32[4096,64]{1,0:T(8,128)}) %all-reduce.5.cloned.1.call-update) | async-done | bytes 1048592 | tf_op jit(solution)/shard_map/psum | solution.py:57
  585.1 5.9 fusion.69
  591.0 24.4 %psum.31 = f32[64,64]{0,1:T(8,128)S(1)} all-reduce(f32[64,64]{0,1:T(8,128)S(1)} %fusion.69), channel_id=1, replica_groups=mesh['wide'=8,'by'=4] {'wide'}, use_global_device_ids=true, to_apply=%region_7.10 | all-reduce | flops 4096 | bytes 32768 | tf_op jit(solution)/shard_map/psum | solution.py:58
  615.5 5.8 cholesky.55
  (77 shorter events, 135.4 us)
Async XLA Ops:
  8.8 54.4 %all-to-all-start = ((s32[8,1,3]{2,1,0:T(1,128)}), s32[8,1,3]{2,1,0:T(1,128)S(1)}, u32[]{:S(2)}, u32[]{:S(2)}) async-start(s32[8,1,3]{2,1,0:T(1,128)} %bitcast.1), calls=%async_computation | async-start | bytes 8192 | tf_op jit(solution)/shard_map/all_to_all | solution.py:28
  16.5 4.7 copy-start.2
  63.2 53.7 %all-to-all-start.2 = ((f32[8,3,32768]{2,1,0:T(4,128)}), f32[8,3,32768]{2,1,0:T(4,128)}, u32[]{:S(2)}, u32[]{:S(2)}) async-start(f32[8,3,32768]{2,1,0:T(4,128)} %copy.60), calls=%async_computation.2 | async-start | bytes 8388608 | tf_op jit(solution)/shard_map/all_to_all | solution.py:54
  116.9 53.7 %all-to-all-start.1 = ((f32[8,3,32768]{2,1,0:T(4,128)}), f32[8,3,32768]{2,1,0:T(4,128)}, u32[]{:S(2)}, u32[]{:S(2)}) async-start(f32[8,3,32768]{2,1,0:T(4,128)} %copy.53), calls=%async_computation.1 | async-start | bytes 8388608 | tf_op jit(solution)/shard_map/all_to_all | solution.py:40
  121.4 205.1 %all-reduce.3.cloned.1.call-start = ((), (), s32[]{:S(2)}) async-start(), calls=%async_computation.5 | async-start | bytes 4194304 | tf_op jit(solution)/shard_map/psum | solution.py:57
  326.6 42.5 %copy-start.1 = (f32[4096,64]{1,0:T(8,128)S(1)}, f32[4096,64]{1,0:T(8,128)}, u32[]{:S(2)}) copy-start(f32[4096,64]{1,0:T(8,128)} %all-reduce.3.cloned.1.call-done) | copy-start | bytes 3145732
  378.2 54.0 %all-to-all-start.3 = ((f32[8,3,32768]{2,1,0:T(4,128)}), f32[8,3,32768]{2,1,0:T(4,128)}, u32[]{:S(2)}, u32[]{:S(2)}) async-start(f32[8,3,32768]{2,1,0:T(4,128)} %copy.64), calls=%async_computation.3 | async-start | bytes 8388608 | tf_op jit(solution)/shard_map/all_to_all | solution.py:40
  432.2 56.1 %all-to-all-start.4 = ((f32[8,3,32768]{2,1,0:T(4,128)}), f32[8,3,32768]{2,1,0:T(4,128)}, u32[]{:S(2)}, u32[]{:S(2)}) async-start(f32[8,3,32768]{2,1,0:T(4,128)} %copy.71), calls=%async_computation.4 | async-start | bytes 8388608 | tf_op jit(solution)/shard_map/all_to_all | solution.py:54
  436.7 148.4 %all-reduce.5.cloned.1.call-start = ((), (), s32[]{:S(2)}) async-start(), calls=%async_computation.6 | async-start | bytes 4194304 | tf_op jit(solution)/shard_map/psum | solution.py:57
  585.1 43.1 %copy-start = (f32[4096,64]{1,0:T(8,128)S(1)}, f32[4096,64]{1,0:T(8,128)}, u32[]{:S(2)}) copy-start(f32[4096,64]{1,0:T(8,128)} %all-reduce.5.cloned.1.call-done) | copy-start | bytes 3145732
Sparse Core Ops, SparseCore 0:
  240.6 85.9 all-reduce.2
  499.0 86.0 all-reduce.4
where the time goes:
time: 648 us; the launch traced here: 639 us
  waiting for transfers between devices  271 us (42%)
  matrix products  138 us (21%)
  local copies, waits for them, and re-layouts  116 us (18%)
  blocking collectives  48.7 us (8%)
  other arithmetic  26.4 us (4%)
  starting transfers between devices  23.7 us (4%)
  between operations  14.6 us (2%)
    psum x2, waiting for transfers between devices, local(): image = lax.psum(partial_rows, 'by')  172 us
    all_to_all x2, waiting for transfers between devices, local(): lax.all_to_all(outgoing, 'wide', split_axis=0, concat_axis=0, tiled=True)  56.9 us
    dot_general x2, matrix products, local(): direct = jnp.einsum('tab,tbk->tak', tiles, col_panels, precision=highest)  52.9 us
    psum x2, blocking collectives, local(): gram = lax.psum(jnp.dot(image.T, image, precision=highest), 'wide')  48.7 us
    all_to_all x2, waiting for transfers between devices, local(): lax.all_to_all(placed, 'wide', split_axis=0, concat_axis=0, tiled=True)  41.6 us
    dot_general x2, matrix products, local(): mirror = jnp.einsum('tba,tbk->tak', tiles, row_panels, precision=highest)  40.7 us
    dot_general x4, local copies, waits for them, and re-layouts, local(): jnp.dot(slot_table, received, precision=highest)  22.9 us
    another operation x6, other arithmetic, local(): factor = jnp.linalg.cholesky(gram)  13 us
  transfers between devices with their start and end apart: 7, of which 5 were waited for; matrix products, arithmetic and copies ran while one was open for 22% of the time, Pallas kernels for 0%

commit v1 on v0

--- a/solution.py
+++ b/solution.py
@@ -55,7 +55,7 @@
         partial_rows = partial_rows + jnp.dot(serve_table.T, returned, precision=highest)
         partial_rows = partial_rows.reshape(block_rows * block_size, width)
         image = lax.psum(partial_rows, "by")
-        gram = lax.psum(jnp.dot(image.T, image, precision=highest), "wide")
+        gram = jnp.sum(lax.all_gather(jnp.dot(image.T, image, precision=highest), "wide"), axis=0)
         factor = jnp.linalg.cholesky(gram)
         panel = jax.scipy.linalg.solve_triangular(factor, image.T, lower=True).T
     return (panel, factor)

time: 648 us -> 618 us (0.954)
  blocking collectives: 48.7 us -> 18.9 us
    psum x2 -> x0, blocking collectives: 48.7 us -> none  [local(): gram = lax.psum(jnp.dot(image.T, image, precision=highest), 'wide')]
    all_gather x0 -> x2, blocking collectives: none -> 18.9 us  [local(): lax.all_gather(jnp.dot(image.T, image, precision=highest), 'wide')]
  transfers between devices with their start and end apart: 7 -> 7, of which waited for: 5 -> 5; matrix products, arithmetic and copies ran while one was open for 22% -> 23% of each run, Pallas kernels for 0% -> 0%
where the time goes in v1:
time: 618 us; the launch traced here: 609 us
  waiting for transfers between devices  271 us (44%)
  matrix products  138 us (22%)
  local copies, waits for them, and re-layouts  116 us (19%)
  other arithmetic  26.4 us (4%)
  starting transfers between devices  23.7 us (4%)
  blocking collectives  18.9 us (3%)
  between operations  14.6 us (2%)
    psum x2, waiting for transfers between devices, local(): image = lax.psum(partial_rows, 'by')  172 us
    all_to_all x2, waiting for transfers between devices, local(): lax.all_to_all(outgoing, 'wide', split_axis=0, concat_axis=0, tiled=True)  56.9 us
    dot_general x2, matrix products, local(): direct = jnp.einsum('tab,tbk->tak', tiles, col_panels, precision=highest)  52.9 us
    all_to_all x2, waiting for transfers between devices, local(): lax.all_to_all(placed, 'wide', split_axis=0, concat_axis=0, tiled=True)  41.6 us
    dot_general x2, matrix products, local(): mirror = jnp.einsum('tba,tbk->tak', tiles, row_panels, precision=highest)  40.7 us
    dot_general x4, local copies, waits for them, and re-layouts, local(): jnp.dot(slot_table, received, precision=highest)  22.9 us
    all_gather x2, blocking collectives, local(): lax.all_gather(jnp.dot(image.T, image, precision=highest), 'wide')  18.9 us
    another operation x6, other arithmetic, local(): factor = jnp.linalg.cholesky(gram)  13 us
  transfers between devices with their start and end apart: 7, of which 5 were waited for; matrix products, arithmetic and copies ran while one was open for 23% of the time, Pallas kernels for 0%

profile of v1, /device:TPU:0, one launch (start us, length us, event | category | flops | bytes accessed | tf_op | source)
XLA Modules:
  0.0 608.6 jit_solution(606154744110531305)
XLA Ops:
  8.8 5.2 all-to-all-start
  22.6 21.3 %fusion.13 = f32[22,512,64]{1,2,0:T(8,128)} fusion(f32[22,512,512]{2,1,0:T(8,128)} %param.7, f32[22,512,64]{1,0,2:T(8,128)S(1)} %fusion.60), kind=kOutput, calls=%fused_computation.15 | convolution fusion | flops 4429185024 | bytes 28835840 | tf_op jit(solution)/shard_map/tba,tbk->tak/dot_general | solution.py:48
  43.9 5.3 copy.53
  49.2 6.3 %reshape.155 = f32[22,32768,1]{1,0,2:T(8,128)} reshape(f32[22,512,64]{2,1,0:T(8,128)} %copy.53) | data formatting | bytes 5767168 | tf_op jit(solution)/shard_map/reshape | solution.py:52
  75.3 41.6 %all-to-all-done.2 = f32[8,3,32768]{2,1,0:T(4,128)} async-done(((f32[8,3,32768]{2,1,0:T(4,128)}), f32[8,3,32768]{2,1,0:T(4,128)}, u32[]{:S(2)}, u32[]{:S(2)}) %all-to-all-start.2) | async-done | bytes 3145760 | tf_op jit(solution)/shard_map/all_to_all | solution.py:54
  125.3 45.2 %all-to-all-done.1 = f32[8,3,32768]{2,1,0:T(4,128)} async-done(((f32[8,3,32768]{2,1,0:T(4,128)}), f32[8,3,32768]{2,1,0:T(4,128)}, u32[]{:S(2)}, u32[]{:S(2)}) %all-to-all-start.1) | async-done | bytes 3145760 | tf_op jit(solution)/shard_map/all_to_all | solution.py:40
  170.5 5.5 all_to_all.30
  176.0 6.4 %dot_general.80 = f32[512,64,24]{1,0,2:T(8,128)} reshape(f32[32768,24]{0,1:T(8,128)} %bitcast.84) | data formatting | bytes 6291456 | tf_op jit(solution)/shard_map/dot_general | solution.py:41
  182.4 6.6 %copy.48 = f32[512,64,24]{0,2,1:T(8,128)} copy(f32[512,64,24]{1,0,2:T(8,128)} %dot_general.80) | data formatting | bytes 6291456 | tf_op jit(solution)/shard_map/dot_general | solution.py:41
  192.6 27.3 %fusion.10 = f32[22,512,64]{1,2,0:T(8,128)} fusion(f32[22,512,512]{2,1,0:T(8,128)} %param.7, f32[22,512,64]{1,0,2:T(8,128)S(1)} %fusion.37), kind=kOutput, calls=%fused_computation.14 | convolution fusion | flops 4429185024 | bytes 28835840 | tf_op jit(solution)/shard_map/tab,tbk->tak/dot_general | solution.py:47
  219.9 5.3 copy.50
  225.3 6.5 %reshape.143 = f32[22,32768]{1,0:T(8,128)} reshape(f32[22,512,64]{2,1,0:T(8,128)} %copy.50) | data formatting | bytes 5767168 | tf_op jit(solution)/shard_map/reshape | solution.py:50
  240.5 86.1 %all-reduce.3.cloned.1.call-done = f32[4096,64]{1,0:T(8,128)} async-done(((f32[4096,64]{1,0:T(8,128)}), f32[4096,64]{1,0:T(8,128)}) %all-reduce.3.cloned.1.call-update) | async-done | bytes 1048592 | tf_op jit(solution)/shard_map/psum | solution.py:57
  326.6 5.9 fusion.68
  332.5 9.4 %all-gather = f32[512,64]{1,0:T(8,128)S(1)} all-gather(f32[64,64]{1,0:T(8,128)S(1)} %fusion.68), channel_id=2, replica_groups=mesh['wide'=8,'by'=4] {'wide'}, dimensions={0}, use_global_device_ids=true | all-gather | bytes 147456 | tf_op jit(solution)/shard_map/all_gather | solution.py:58
  342.1 5.8 cholesky.44
  372.0 19.4 %fusion.19 = f32[22,512,64]{1,2,0:T(8,128)S(1)} fusion(f32[22,512,512]{2,1,0:T(8,128)} %param.7, f32[22,512,64]{1,0,2:T(8,128)S(1)} %fusion.58), kind=kOutput, calls=%fused_computation.17 | convolution fusion | flops 4429185024 | bytes 28835840 | tf_op jit(solution)/shard_map/tba,tbk->tak/dot_general | solution.py:48
  405.7 11.6 %all-to-all-done.3 = f32[8,3,32768]{2,1,0:T(4,128)} async-done(((f32[8,3,32768]{2,1,0:T(4,128)}), f32[8,3,32768]{2,1,0:T(4,128)}, u32[]{:S(2)}, u32[]{:S(2)}) %all-to-all-start.3) | async-done | bytes 3145760 | tf_op jit(solution)/shard_map/all_to_all | solution.py:40
  430.6 5.0 copy.58
  437.3 25.6 %fusion.16 = f32[22,512,64]{1,2,0:T(8,128)S(1)} fusion(f32[22,512,512]{2,1,0:T(8,128)} %param.7, f32[22,512,64]{1,0,2:T(8,128)S(1)} %fusion.35), kind=kOutput, calls=%fused_computation.16 | convolution fusion | flops 4429185024 | bytes 28835840 | tf_op jit(solution)/shard_map/tab,tbk->tak/dot_general | solution.py:47
  484.0 86.0 %all-reduce.5.cloned.1.call-done = f32[4096,64]{1,0:T(8,128)} async-done(((f32[4096,64]{1,0:T(8,128)}), f32[4096,64]{1,0:T(8,128)}) %all-reduce.5.cloned.1.call-update) | async-done | bytes 1048592 | tf_op jit(solution)/shard_map/psum | solution.py:57
  570.0 5.9 fusion.69
  576.0 9.5 %all-gather.1 = f32[512,64]{1,0:T(8,128)S(1)} all-gather(f32[64,64]{1,0:T(8,128)S(1)} %fusion.69), channel_id=3, replica_groups=mesh['wide'=8,'by'=4] {'wide'}, dimensions={0}, use_global_device_ids=true | all-gather | bytes 147456 | tf_op jit(solution)/shard_map/all_gather | solution.py:58
  585.6 5.8 cholesky.55
  (79 shorter events, 135.4 us)
Async XLA Ops:
  8.8 54.4 %all-to-all-start = ((s32[8,1,3]{2,1,0:T(1,128)}), s32[8,1,3]{2,1,0:T(1,128)S(1)}, u32[]{:S(2)}, u32[]{:S(2)}) async-start(s32[8,1,3]{2,1,0:T(1,128)} %bitcast.1), calls=%async_computation | async-start | bytes 8192 | tf_op jit(solution)/shard_map/all_to_all | solution.py:28
  16.5 4.7 copy-start.2
  63.2 53.7 %all-to-all-start.2 = ((f32[8,3,32768]{2,1,0:T(4,128)}), f32[8,3,32768]{2,1,0:T(4,128)}, u32[]{:S(2)}, u32[]{:S(2)}) async-start(f32[8,3,32768]{2,1,0:T(4,128)} %copy.54), calls=%async_computation.2 | async-start | bytes 8388608 | tf_op jit(solution)/shard_map/all_to_all | solution.py:54
  116.9 53.7 %all-to-all-start.1 = ((f32[8,3,32768]{2,1,0:T(4,128)}), f32[8,3,32768]{2,1,0:T(4,128)}, u32[]{:S(2)}, u32[]{:S(2)}) async-start(f32[8,3,32768]{2,1,0:T(4,128)} %copy.47), calls=%async_computation.1 | async-start | bytes 8388608 | tf_op jit(solution)/shard_map/all_to_all | solution.py:40
  121.4 205.1 %all-reduce.3.cloned.1.call-start = ((), (), s32[]{:S(2)}) async-start(), calls=%async_computation.5 | async-start | bytes 4194304 | tf_op jit(solution)/shard_map/psum | solution.py:57
  326.6 27.6 %copy-start.1 = (f32[4096,64]{1,0:T(8,128)S(1)}, f32[4096,64]{1,0:T(8,128)}, u32[]{:S(2)}) copy-start(f32[4096,64]{1,0:T(8,128)} %all-reduce.3.cloned.1.call-done) | copy-start | bytes 3145732
  363.4 54.0 %all-to-all-start.3 = ((f32[8,3,32768]{2,1,0:T(4,128)}), f32[8,3,32768]{2,1,0:T(4,128)}, u32[]{:S(2)}, u32[]{:S(2)}) async-start(f32[8,3,32768]{2,1,0:T(4,128)} %copy.57), calls=%async_computation.3 | async-start | bytes 8388608 | tf_op jit(solution)/shard_map/all_to_all | solution.py:40
  417.3 56.1 %all-to-all-start.4 = ((f32[8,3,32768]{2,1,0:T(4,128)}), f32[8,3,32768]{2,1,0:T(4,128)}, u32[]{:S(2)}, u32[]{:S(2)}) async-start(f32[8,3,32768]{2,1,0:T(4,128)} %copy.64), calls=%async_computation.4 | async-start | bytes 8388608 | tf_op jit(solution)/shard_map/all_to_all | solution.py:54
  421.9 148.2 %all-reduce.5.cloned.1.call-start = ((), (), s32[]{:S(2)}) async-start(), calls=%async_computation.6 | async-start | bytes 4194304 | tf_op jit(solution)/shard_map/psum | solution.py:57
  570.0 28.2 %copy-start = (f32[4096,64]{1,0:T(8,128)S(1)}, f32[4096,64]{1,0:T(8,128)}, u32[]{:S(2)}) copy-start(f32[4096,64]{1,0:T(8,128)} %all-reduce.5.cloned.1.call-done) | copy-start | bytes 3145732
Sparse Core Ops, SparseCore 0:
  240.6 85.9 all-reduce.2
  484.2 85.8 all-reduce.4
